TPU v7x, 32 devices: a whole 2x2x4 slice. The times are simulated.
32 devices in a mesh: gx: 4 (over z), gy: 8 (over y, x, core).
Axes of the slice: x: 2, y: 2, z: 4, core: 2. Of those that a mesh axis runs over, the one named last changes fastest.
Arguments:
- residual_in: float32 [3, 32, 64, 128], P(None, 'gx', 'gy'), may hold values from -24 to 24, as said below
- accumulation: float32 [3, 3, 32, 64, 128], P(None, None, 'gx', 'gy'), may hold values from -2.4 to 8, as said below
- mobility: float32 [3, 3, 32, 64, 128], P(None, None, 'gx', 'gy'), may hold values from -0.9 to 3, as said below
- permeability: float32 [3, 32, 64, 128], P(None, 'gx', 'gy'), may hold values from 0.1 to 10
- fault_near: int32 [4, 8, 1024], P('gx', 'gy'), may hold values from 0 to 8191, as said below
- fault_far: int32 [4, 8, 1024], P('gx', 'gy'), may hold values from 0 to 8191, as said below
- fault_trans: float32 [4, 8, 1024], P('gx', 'gy'), may hold values from 0 to 5, as said below
- well_cells: int32 [4, 8, 2], P('gx', 'gy'), may hold values from 0 to 8191
- well_rates: float32 [4, 8, 2], P('gx', 'gy'), may hold values from 1 to 5
Outputs:
- newton_update: float32 [3, 32, 64, 128], P(None, 'gx', 'gy')
- decoupled_residual: float32 [3, 32, 64, 128], P(None, 'gx', 'gy')
Inputs may be any that keep to these rules, and one draw needn't show every extreme that they name: `accumulation`: each row's off-diagonal entries together are at most 0.6 times its positive diagonal entry. `mobility`: each row's off-diagonal entries together are at most 0.6 times its positive diagonal entry. `fault_near`: a local index of a cell in the last two rows along the second areal dimension of its device's block. `fault_far`: a local index of a cell in the first two rows along the second areal dimension of its device's block. `fault_trans`: at each boundary the live slots come first and the rest are zero; all slots of devices with j = 0 are zero; some boundary uses all 1024 slots. `residual_in`: values at most 24 in magnitude. `well_cells`: a local index of a cell of its device's block.
All inputs are finite; a program needn't handle non-finite values.
Results may differ from a plain program's by a relative error of at most 0.0012.
Values sent between devices are 32-bit elements; how exact they have to be, the bound alone decides.
A program may use at most 64 MiB of HBM per device.

v0:
```python
import functools

import jax
import jax.numpy as jnp
from jax import lax
from jax.experimental import pallas as pl
from jax.experimental.pallas import tpu as pltpu
from jax.sharding import PartitionSpec as P

KRYLOV = 3
PAIRS = [(a, b) for a in range(KRYLOV + 1) for b in range(a, KRYLOV + 1)]
MESH = pl.DeviceIdType.MESH


def harmonic(a, b):
    return 2.0 * a * b / (a + b)


def quotient(value, by):
    if by & (by - 1) == 0:
        return lax.shift_right_logical(value, jnp.int32(by.bit_length() - 1))
    return value // by


def split_two(value):
    high = value.astype(jnp.bfloat16)
    low = (value - high.astype(jnp.float32)).astype(jnp.bfloat16)
    return high, low


def solve_small(matrix, rhs_values):
    size = len(rhs_values)
    rows = [list(line) for line in matrix]
    values = list(rhs_values)
    for column in range(size):
        for lower in range(column + 1, size):
            factor = rows[lower][column] / rows[column][column]
            rows[lower] = [e - factor * p for e, p in zip(rows[lower], rows[column])]
            values[lower] = values[lower] - factor * values[column]
    solved = [0.0] * size
    for column in reversed(range(size)):
        partial = values[column]
        for later in range(column + 1, size):
            partial = partial - rows[column][later] * solved[later]
        solved[column] = partial / rows[column][column]
    return solved


def kernel(
    nx, ny, cx, cy, nz, cap, wells,
    res_h, acc_h, mob_h, perm_h, near_h, far_h, tr_h, wc_ref, wr_ref,
    upd_o, out_o,
    res_v, acc_v, mob_v, perm_v, near_v, far_v, tr_v,
    far_u, tr_u, near_l,
    ps_u, ps_l, py_l, py_u, px_l, px_u,
    tot, inv, mix, w_v, ys, flux, offs,
    send_u, send_l, send_e, send_w, recv_l, recv_u, recv_w, recv_e,
    z_far, z_near, z_near_l, z_far_u,
    red_y, red_x,
    load_sem, s0, r0, s1, r1, sy, ry, sx, rx,
):
    gx, gy = lax.axis_index("gx"), lax.axis_index("gy")
    has_l, has_u = gy > 0, gy < ny - 1
    has_w, has_e = gx > 0, gx < nx - 1

    barrier = pltpu.get_barrier_semaphore()
    for d in range(1, ny):
        pl.semaphore_signal(barrier, inc=1, device_id={"gy": lax.rem(gy + d, ny)}, device_id_type=MESH)
    for d in range(1, nx):
        pl.semaphore_signal(barrier, inc=1, device_id={"gx": lax.rem(gx + d, nx)}, device_id_type=MESH)

    loads = []
    for k, (src, dst) in enumerate([
        (perm_h, perm_v), (near_h, near_v), (far_h, far_v), (tr_h, tr_v),
        (acc_h, acc_v), (mob_h, mob_v), (res_h, res_v),
    ]):
        copy = pltpu.make_async_copy(src, dst, load_sem.at[k])
        copy.start()
        loads.append(copy)

    loads[0].wait()
    perm = perm_v.reshape(3 * cx * cy, nz)
    ps_u[...] = perm[pl.ds(cx * cy + cy - 1, cx, stride=cy), :]
    ps_l[...] = perm[pl.ds(cx * cy, cx, stride=cy), :]
    for k in (1, 2, 3):
        loads[k].wait()

    pl.semaphore_wait(barrier, nx + ny - 2)

    def remote(src, dst, send, recv, target):
        return pltpu.make_async_remote_copy(
            src_ref=src, dst_ref=dst, send_sem=send, recv_sem=recv,
            device_id=target, device_id_type=MESH,
        )

    up, down = {"gy": gy + 1}, {"gy": gy - 1}
    east, west = {"gx": gx + 1}, {"gx": gx - 1}
    first_u = [
        remote(near_v, near_l, s0.at[0], r0.at[0], up),
        remote(ps_u, py_l, s0.at[1], r0.at[1], up),
    ]
    first_l = [
        remote(far_v, far_u, s0.at[2], r0.at[2], down),
        remote(tr_v, tr_u, s0.at[3], r0.at[3], down),
        remote(ps_l, py_u, s0.at[4], r0.at[4], down),
    ]
    first_e = [remote(perm_v.at[0, cx - 1], px_l, s0.at[5], r0.at[5], east)]
    first_w = [remote(perm_v.at[0, 0], px_u, s0.at[6], r0.at[6], west)]

    def start(to_u, to_l, to_e, to_w):
        for flag, copies in ((has_u, to_u), (has_l, to_l), (has_e, to_e), (has_w, to_w)):
            @pl.when(flag)
            def _(copies=copies):
                for copy in copies:
                    copy.start()

    def arrive(to_u, to_l, to_e, to_w):
        for flag, copies in ((has_u, to_l), (has_l, to_u), (has_e, to_w), (has_w, to_e)):
            @pl.when(flag)
            def _(copies=copies):
                for copy in copies:
                    copy.wait_recv()

    def sent(to_u, to_l, to_e, to_w):
        for flag, copies in ((has_u, to_u), (has_l, to_l), (has_e, to_e), (has_w, to_w)):
            @pl.when(flag)
            def _(copies=copies):
                for copy in copies:
                    copy.wait_send()

    start(first_u, first_l, first_e, first_w)

    def clear(flag, *refs):
        @pl.when(jnp.logical_not(flag))
        def _():
            for ref in refs:
                ref[...] = jnp.zeros(ref.shape, ref.dtype)

    clear(has_l, near_l, py_l, recv_l)
    clear(has_u, far_u, tr_u, py_u, recv_u)
    clear(has_w, px_l, recv_w)
    clear(has_e, px_u, recv_e)

    rows = 2 * cx
    row_iota = lax.broadcasted_iota(jnp.int32, (rows, cap), 0)
    layer_iota = lax.broadcasted_iota(jnp.int32, (nz, cap), 0)

    def slots(ref, base, onehot):
        index = ref[...]
        column = quotient(index, nz)
        layer = index - column * nz
        across = quotient(column, cy)
        along = column - across * cy - base
        onehot[...] = jnp.where(layer_iota == layer, 1.0, 0.0).astype(jnp.bfloat16)
        return row_iota == along * cx + across

    far_rows = slots(far_v, 0, z_far)
    near_rows = slots(near_v, cy - 2, z_near)

    def scatter(values, where_rows, onehot):
        parts = []
        for value in values:
            chosen = jnp.where(where_rows, value, 0.0)
            parts.extend(split_two(chosen))
        spread = lax.dot_general(
            jnp.concatenate(parts, axis=0), onehot[...], (((1,), (1,)), ((), ())),
            preferred_element_type=jnp.float32,
        )
        return [
            spread[2 * c * rows:(2 * c + 1) * rows] + spread[(2 * c + 1) * rows:(2 * c + 2) * rows]
            for c in range(len(values))
        ]

    def gather(block, where_rows, onehot):
        high, low = split_two(block)
        found = lax.dot_general(
            jnp.concatenate([high, low], axis=0), onehot[...], (((1,), (0,)), ((), ())),
            preferred_element_type=jnp.float32,
        )
        found = found[:3 * rows] + found[3 * rows:]
        return [
            jnp.sum(jnp.where(where_rows, found[c * rows:(c + 1) * rows], 0.0), axis=0, keepdims=True)
            for c in range(3)
        ]

    trans = tr_v[...]
    perm_x, perm_y, perm_z = perm_v[0], perm_v[1], perm_v[2]
    y_iota = lax.broadcasted_iota(jnp.int32, (cx, cy, nz), 1)
    z_iota = lax.broadcasted_iota(jnp.int32, (cx, cy, nz), 2)
    t_x = harmonic(perm_x[:-1], perm_x[1:])
    t_n = jnp.where(y_iota == cy - 1, 0.0, harmonic(perm_y, pltpu.roll(perm_y, cy - 1, 1)))
    t_s = jnp.where(y_iota == 0, 0.0, harmonic(perm_y, pltpu.roll(perm_y, 1, 1)))
    t_a = jnp.where(z_iota == nz - 1, 0.0, harmonic(perm_z, pltpu.roll(perm_z, nz - 1, 2)))
    t_b = jnp.where(z_iota == 0, 0.0, harmonic(perm_z, pltpu.roll(perm_z, 1, 2)))
    far_sum = scatter([trans], far_rows, z_far)[0]

    arrive(first_u, first_l, first_e, first_w)
    near_rows_l = slots(near_l, cy - 2, z_near_l)
    far_rows_u = slots(far_u, 0, z_far_u)
    trans_u = tr_u[...]
    near_sum = scatter([trans_u], near_rows, z_near)[0]
    t_w0 = harmonic(perm_x[0], px_l[...])
    t_e1 = harmonic(perm_x[cx - 1], px_u[...])
    t_e = jnp.concatenate([t_x, t_e1[None]], axis=0)
    t_w = jnp.concatenate([t_w0[None], t_x], axis=0)
    t_s0 = harmonic(ps_l[...], py_l[...])
    t_n1 = harmonic(ps_u[...], py_u[...])

    flat = cx * cy
    tot[...] = (t_e + t_w + t_n + t_s + t_a + t_b).reshape(flat, nz)

    def add_rows(ref, start_row, value):
        place = (pl.ds(start_row, cx, stride=cy), slice(None))
        ref[place] = ref[place] + value

    add_rows(tot, 0, far_sum[:cx] + t_s0)
    add_rows(tot, 1, far_sum[cx:])
    add_rows(tot, cy - 2, near_sum[:cx])
    add_rows(tot, cy - 1, near_sum[cx:] + t_n1)

    for k in (4, 5, 6):
        loads[k].wait()
    total = tot[...].reshape(cx, cy, nz)
    mob = [[mob_v[a, b] for b in range(3)] for a in range(3)]
    diag = [[acc_v[a, b] + total * mob[a][b] for b in range(3)] for a in range(3)]
    w1 = diag[0][1] / diag[1][1]
    w2 = diag[0][2] / diag[2][2]
    w_v[0] = w1
    w_v[1] = w2
    blk = [[diag[0][b] - w1 * diag[1][b] - w2 * diag[2][b] for b in range(3)], diag[1], diag[2]]

    def part(a, b, c, d):
        return blk[a][b] * blk[c][d] - blk[a][d] * blk[c][b]

    cof = [
        [part(1, 1, 2, 2), -part(1, 0, 2, 2), part(1, 0, 2, 1)],
        [-part(0, 1, 2, 2), part(0, 0, 2, 2), -part(0, 0, 2, 1)],
        [part(0, 1, 1, 2), -part(0, 0, 1, 2), part(0, 0, 1, 1)],
    ]
    det = blk[0][0] * cof[0][0] + blk[0][1] * cof[0][1] + blk[0][2] * cof[0][2]
    inverse_det = 1.0 / det
    pre = [[cof[b][a] * inverse_det for b in range(3)] for a in range(3)]
    for a in range(3):
        for b in range(3):
            inv[a, b] = pre[a][b]
            mix[a, b] = mob[a][0] * pre[0][b] + mob[a][1] * pre[1][b] + mob[a][2] * pre[2][b]

    lin = (
        lax.broadcasted_iota(jnp.int32, (cx, cy, nz), 0) * (cy * nz) + y_iota * nz + z_iota
    )
    rhs0, rhs1, rhs2 = -res_v[0], -res_v[1], -res_v[2]
    for w in range(wells):
        rhs1 = rhs1 + jnp.where(lin == wc_ref[0, w], wr_ref[0, w], 0.0)
    ys[0, 0] = rhs0 - w1 * rhs1 - w2 * rhs2
    ys[0, 1] = rhs1
    ys[0, 2] = rhs2

    pending = [(first_u, first_l, first_e, first_w)]
    for it in range(KRYLOV):
        y = [ys[it, c] for c in range(3)]
        field = []
        for a in range(3):
            value = mix[a, 0] * y[0] + mix[a, 1] * y[1] + mix[a, 2] * y[2]
            field.append(value)
            flux[pl.ds(a * flat, flat), :] = value.reshape(flat, nz)
            send_e[it, a] = value[cx - 1]
            send_w[it, a] = value[0]
        for a in range(3):
            for r in range(2):
                at = pl.ds((2 * a + r) * cx, cx)
                send_u[it, at, :] = flux[pl.ds(a * flat + cy - 2 + r, cx, stride=cy), :]
                send_l[it, at, :] = flux[pl.ds(a * flat + r, cx, stride=cy), :]
        copies = (
            [remote(send_u.at[it], recv_l.at[it], s1.at[it, 0], r1.at[it, 0], up)],
            [remote(send_l.at[it], recv_u.at[it], s1.at[it, 1], r1.at[it, 1], down)],
            [remote(send_e.at[it], recv_w.at[it], s1.at[it, 2], r1.at[it, 2], east)],
            [remote(send_w.at[it], recv_e.at[it], s1.at[it, 3], r1.at[it, 3], west)],
        )
        start(*copies)
        pending.append(copies)
        inner = []
        for a in range(3):
            f = field[a]
            near_sums = (
                t_n * pltpu.roll(f, cy - 1, 1) + t_s * pltpu.roll(f, 1, 1)
                + t_a * pltpu.roll(f, nz - 1, 2) + t_b * pltpu.roll(f, 1, 2)
            )
            inner.append(near_sums)
        arrive(*copies)
        below, above = recv_l[it], recv_u[it]
        got_l = gather(below, near_rows_l, z_near_l)
        got_u = gather(above, far_rows_u, z_far_u)
        fault_l = scatter([trans * g for g in got_l], far_rows, z_far)
        fault_u = scatter([trans_u * g for g in got_u], near_rows, z_near)
        for a in range(3):
            f = field[a]
            value = (
                inner[a]
                + t_e * jnp.concatenate([f[1:], recv_e[it, a][None]], axis=0)
                + t_w * jnp.concatenate([recv_w[it, a][None], f[:-1]], axis=0)
            )
            offs[pl.ds(a * flat, flat), :] = value.reshape(flat, nz)
            halo_s = below[(2 * a + 1) * cx:(2 * a + 2) * cx]
            halo_n = above[2 * a * cx:(2 * a + 1) * cx]
            add_rows(offs, a * flat, fault_l[a][:cx] + t_s0 * halo_s)
            add_rows(offs, a * flat + 1, fault_l[a][cx:])
            add_rows(offs, a * flat + cy - 2, fault_u[a][:cx])
            add_rows(offs, a * flat + cy - 1, fault_u[a][cx:] + t_n1 * halo_n)
        o = [offs[pl.ds(a * flat, flat), :].reshape(cx, cy, nz) for a in range(3)]
        ys[it + 1, 0] = y[0] - (o[0] - w_v[0] * o[1] - w_v[1] * o[2])
        ys[it + 1, 1] = y[1] - o[1]
        ys[it + 1, 2] = y[2] - o[2]

    count = red_y.shape[1]
    lines = []
    for left, right in PAIRS:
        lines.append(
            jnp.sum(jnp.sum(ys[left] * ys[right], axis=(0, 1)), axis=0, keepdims=True)
        )
    lines.append(jnp.zeros((count - len(PAIRS), nz), jnp.float32))
    red_y[gy] = jnp.concatenate(lines, axis=0)
    around = [
        remote(red_y.at[gy], red_y.at[gy], sy.at[d], ry.at[d], {"gy": lax.rem(gy + d, ny)})
        for d in range(1, ny)
    ]
    for copy in around:
        copy.start()
    for copy in around:
        copy.wait_recv()
    partial = red_y[0]
    for d in range(1, ny):
        partial = partial + red_y[d]
    red_x[gx] = partial
    across = [
        remote(red_x.at[gx], red_x.at[gx], sx.at[d], rx.at[d], {"gx": lax.rem(gx + d, nx)})
        for d in range(1, nx)
    ]
    for copy in across:
        copy.start()
    for copy in across:
        copy.wait_recv()
    partial = red_x[0]
    for d in range(1, nx):
        partial = partial + red_x[d]
    sums = jnp.broadcast_to(jnp.sum(partial, axis=1, keepdims=True), partial.shape)

    def entry(left, right):
        k = PAIRS.index((min(left, right), max(left, right)))
        return sums[k:k + 1]

    normal = [[entry(a + 1, b + 1) for b in range(KRYLOV)] for a in range(KRYLOV)]
    coefs = solve_small(normal, [entry(0, a + 1) for a in range(KRYLOV)])
    coefs = [c.reshape(1, 1, nz) for c in coefs]
    mixed = []
    for c in range(3):
        combined = coefs[0] * ys[0, c]
        applied = coefs[0] * ys[1, c]
        for k in range(1, KRYLOV):
            combined = combined + coefs[k] * ys[k, c]
            applied = applied + coefs[k] * ys[k + 1, c]
        mixed.append(combined)
        out_o[c] = ys[0, c] - applied
    for c in range(3):
        upd_o[c] = inv[c, 0] * mixed[0] + inv[c, 1] * mixed[1] + inv[c, 2] * mixed[2]
    for group in pending:
        sent(*group)
    for copy in around + across:
        copy.wait_send()


def solution(mesh):
    nx, ny = mesh.shape["gx"], mesh.shape["gy"]
    placed = (
        P(None, "gx", "gy", None),
        P(None, None, "gx", "gy", None),
        P(None, None, "gx", "gy", None),
        P(None, "gx", "gy", None),
    ) + (P("gx", "gy", None),) * 5

    def shards(residual_in, accumulation, mobility, permeability, fault_near, fault_far, fault_trans, well_cells, well_rates):
        _, cx, cy, nz = residual_in.shape
        cap = fault_near.shape[-1]
        wells = well_cells.shape[-1]
        flat = cx * cy
        lines = -(-len(PAIRS) // 8) * 8
        f32, i32, bf16 = jnp.float32, jnp.int32, jnp.bfloat16
        vm = pltpu.VMEM
        dma = pltpu.SemaphoreType.DMA
        scratch = [
            vm((3, cx, cy, nz), f32), vm((3, 3, cx, cy, nz), f32), vm((3, 3, cx, cy, nz), f32),
            vm((3, cx, cy, nz), f32),
            vm((1, cap), i32), vm((1, cap), i32), vm((1, cap), f32),
            vm((1, cap), i32), vm((1, cap), f32), vm((1, cap), i32),
        ]
        scratch += [vm((cx, nz), f32)] * 4 + [vm((cy, nz), f32)] * 2
        scratch += [
            vm((flat, nz), f32), vm((3, 3, cx, cy, nz), f32), vm((3, 3, cx, cy, nz), f32),
            vm((2, cx, cy, nz), f32), vm((KRYLOV + 1, 3, cx, cy, nz), f32),
            vm((3 * flat, nz), f32), vm((3 * flat, nz), f32),
        ]
        scratch += [vm((KRYLOV, 6 * cx, nz), f32)] * 2 + [vm((KRYLOV, 3, cy, nz), f32)] * 2
        scratch += [vm((KRYLOV, 6 * cx, nz), f32)] * 2 + [vm((KRYLOV, 3, cy, nz), f32)] * 2
        scratch += [vm((nz, cap), bf16)] * 4
        scratch += [vm((ny, lines, nz), f32), vm((nx, lines, nz), f32)]
        scratch += [
            dma((7,)), dma((7,)), dma((7,)), dma((KRYLOV, 4)), dma((KRYLOV, 4)),
            dma((ny,)), dma((ny,)), dma((nx,)), dma((nx,)),
        ]
        anywhere = pl.BlockSpec(memory_space=pl.ANY)
        scalars = pl.BlockSpec(memory_space=pltpu.SMEM)
        inside = pl.BlockSpec(memory_space=pltpu.VMEM)
        shape = jax.ShapeDtypeStruct(residual_in.shape, f32)
        return pl.pallas_call(
            functools.partial(kernel, nx, ny, cx, cy, nz, cap, wells),
            out_shape=(shape, shape),
            in_specs=[anywhere] * 7 + [scalars] * 2,
            out_specs=(inside, inside),
            scratch_shapes=scratch,
            compiler_params=pltpu.CompilerParams(collective_id=0, has_side_effects=True),
            name="newton",
        )(
            residual_in, accumulation, mobility, permeability,
            fault_near.reshape(1, cap), fault_far.reshape(1, cap), fault_trans.reshape(1, cap),
            well_cells.reshape(1, wells), well_rates.reshape(1, wells),
        )

    out = P(None, "gx", "gy", None)
    return jax.shard_map(shards, mesh=mesh, in_specs=placed, out_specs=(out, out), check_vma=False)
```

profile of v0, /device:TPU:0, one launch (start us, length us, event | category | flops | bytes accessed | tf_op | source)
XLA Modules:
  0.0 30.5 jit_solution(17548860618145912880)
XLA Ops:
  0.6 27.6 %newton.1 = (f32[3,8,8,128]{3,2,1,0:T(8,128)}, f32[3,8,8,128]{3,2,1,0:T(8,128)}) custom-call(f32[3,8,8,128]{3,2,1,0:T(8,128)} %res_h.1, f32[3,3,8,8,128]{4,3,2,1,0:T(8,128)} %acc_h.1, f32[3,3,8,8,128]{4,3,2,1,0:T(8,128)} %mob_h.1, f32[3,8,8,128]{3,2,1,0:T(8,128)} %perm_h.1, s32[1,1024]{1,0:T(1,128)} %bitcast.5, s32[1,1024]{1,0:T(1,128)} %bitcast.6, ...), custom_call_target="tpu_custom_call" | custom-call | tf_op jit(solution)/shard_map/newton/pallas_call | solution.py:413
  28.2 0.0 copy-start
  28.2 1.6 %copy.13 = f32[3,8,8,128]{3,2,1,0:T(8,128)} copy(f32[3,8,8,128]{3,2,1,0:T(8,128)} %get-tuple-element.4) | data formatting | bytes 196608
  29.8 0.0 copy-done
  29.8 0.6 %copy.14 = f32[3,8,8,128]{3,2,1,0:T(8,128)} copy(f32[3,8,8,128]{3,2,1,0:T(8,128)S(1)} %copy-done) | data formatting | bytes 196608
Async XLA Ops:
  28.2 1.6 %copy-start = (f32[3,8,8,128]{3,2,1,0:T(8,128)S(1)}, f32[3,8,8,128]{3,2,1,0:T(8,128)}, u32[]{:S(2)}) copy-start(f32[3,8,8,128]{3,2,1,0:T(8,128)} %get-tuple-element.5) | copy-start | bytes 294916
where the time goes:
time: 30.6 us; the launch traced here: 30.5 us
  Pallas kernels  27.6 us (90%)
  local copies, waits for them, and re-layouts  2.22 us (7%)
  between operations  0.65 us (2%)
    pallas_call x1, Pallas kernels, shards(): pl.pallas_call(functools.partial(kernel, nx, ny, cx, cy, nz, cap, wells),...  27.6 us
    unnamed x4, local copies, waits for them, and re-layouts  2.22 us

commit v1 on v0

--- a/solution.py
+++ b/solution.py
@@ -8,7 +8,7 @@
 from jax.sharding import PartitionSpec as P
 
 KRYLOV = 3
-PAIRS = [(a, b) for a in range(KRYLOV + 1) for b in range(a, KRYLOV + 1)]
+PAIRS = [(a, b) for b in range(KRYLOV + 1) for a in range(b + 1)]
 MESH = pl.DeviceIdType.MESH
 
 
@@ -47,10 +47,11 @@
 
 
 def kernel(
-    nx, ny, cx, cy, nz, cap, wells,
-    res_h, acc_h, mob_h, perm_h, near_h, far_h, tr_h, wc_ref, wr_ref,
+    nx, ny, cx, cy, nz, cap, wells, direct,
+    res_h, acc_h, mob_h, perm_h, near_h, far_h, tr_h, wc_h, wr_h,
     upd_o, out_o,
     res_v, acc_v, mob_v, perm_v, near_v, far_v, tr_v,
+    wc_ref, wr_ref,
     far_u, tr_u, near_l,
     ps_u, ps_l, py_l, py_u, px_l, px_u,
     tot, inv, mix, w_v, ys, flux, offs,
@@ -66,13 +67,22 @@
     barrier = pltpu.get_barrier_semaphore()
     for d in range(1, ny):
         pl.semaphore_signal(barrier, inc=1, device_id={"gy": lax.rem(gy + d, ny)}, device_id_type=MESH)
-    for d in range(1, nx):
-        pl.semaphore_signal(barrier, inc=1, device_id={"gx": lax.rem(gx + d, nx)}, device_id_type=MESH)
+    if direct:
+        for flag, other in ((has_w, gx - 1), (has_e, gx + 1)):
+            @pl.when(flag)
+            def _(other=other):
+                pl.semaphore_signal(barrier, inc=1, device_id={"gx": other}, device_id_type=MESH)
+        greeted = ny - 1 + has_w.astype(jnp.int32) + has_e.astype(jnp.int32)
+    else:
+        for d in range(1, nx):
+            pl.semaphore_signal(barrier, inc=1, device_id={"gx": lax.rem(gx + d, nx)}, device_id_type=MESH)
+        greeted = nx + ny - 2
 
     loads = []
     for k, (src, dst) in enumerate([
         (perm_h, perm_v), (near_h, near_v), (far_h, far_v), (tr_h, tr_v),
         (acc_h, acc_v), (mob_h, mob_v), (res_h, res_v),
+        (wc_h, wc_ref), (wr_h, wr_ref),
     ]):
         copy = pltpu.make_async_copy(src, dst, load_sem.at[k])
         copy.start()
@@ -85,7 +95,7 @@
     for k in (1, 2, 3):
         loads[k].wait()
 
-    pl.semaphore_wait(barrier, nx + ny - 2)
+    pl.semaphore_wait(barrier, greeted)
 
     def remote(src, dst, send, recv, target):
         return pltpu.make_async_remote_copy(
@@ -194,9 +204,15 @@
     t_b = jnp.where(z_iota == 0, 0.0, harmonic(perm_z, pltpu.roll(perm_z, 1, 2)))
     far_sum = scatter([trans], far_rows, z_far)[0]
 
+    for k in range(4, 9):
+        loads[k].wait()
+    lin = (
+        lax.broadcasted_iota(jnp.int32, (cx, cy, nz), 0) * (cy * nz) + y_iota * nz + z_iota
+    )
+    rhs0, rhs1, rhs2 = -res_v[0], -res_v[1], -res_v[2]
+    for w in range(wells):
+        rhs1 = rhs1 + jnp.where(lin == wc_ref[0, w], wr_ref[0, w], 0.0)
     arrive(first_u, first_l, first_e, first_w)
-    near_rows_l = slots(near_l, cy - 2, z_near_l)
-    far_rows_u = slots(far_u, 0, z_far_u)
     trans_u = tr_u[...]
     near_sum = scatter([trans_u], near_rows, z_near)[0]
     t_w0 = harmonic(perm_x[0], px_l[...])
@@ -218,8 +234,6 @@
     add_rows(tot, cy - 2, near_sum[:cx])
     add_rows(tot, cy - 1, near_sum[cx:] + t_n1)
 
-    for k in (4, 5, 6):
-        loads[k].wait()
     total = tot[...].reshape(cx, cy, nz)
     mob = [[mob_v[a, b] for b in range(3)] for a in range(3)]
     diag = [[acc_v[a, b] + total * mob[a][b] for b in range(3)] for a in range(3)]
@@ -245,15 +259,12 @@
             inv[a, b] = pre[a][b]
             mix[a, b] = mob[a][0] * pre[0][b] + mob[a][1] * pre[1][b] + mob[a][2] * pre[2][b]
 
-    lin = (
-        lax.broadcasted_iota(jnp.int32, (cx, cy, nz), 0) * (cy * nz) + y_iota * nz + z_iota
-    )
-    rhs0, rhs1, rhs2 = -res_v[0], -res_v[1], -res_v[2]
-    for w in range(wells):
-        rhs1 = rhs1 + jnp.where(lin == wc_ref[0, w], wr_ref[0, w], 0.0)
     ys[0, 0] = rhs0 - w1 * rhs1 - w2 * rhs2
     ys[0, 1] = rhs1
     ys[0, 2] = rhs2
+
+    def product(left, right):
+        return jnp.sum(jnp.sum(ys[left] * ys[right], axis=(0, 1)), axis=0, keepdims=True)
 
     pending = [(first_u, first_l, first_e, first_w)]
     for it in range(KRYLOV):
@@ -278,6 +289,9 @@
         )
         start(*copies)
         pending.append(copies)
+        if it == 0:
+            near_rows_l = slots(near_l, cy - 2, z_near_l)
+            far_rows_u = slots(far_u, 0, z_far_u)
         inner = []
         for a in range(3):
             f = field[a]
@@ -286,6 +300,8 @@
                 + t_a * pltpu.roll(f, nz - 1, 2) + t_b * pltpu.roll(f, 1, 2)
             )
             inner.append(near_sums)
+        if it == KRYLOV - 1:
+            rows_early = [product(left, right) for left, right in PAIRS if right < KRYLOV]
         arrive(*copies)
         below, above = recv_l[it], recv_u[it]
         got_l = gather(below, near_rows_l, z_near_l)
@@ -307,64 +323,89 @@
             add_rows(offs, a * flat + cy - 2, fault_u[a][:cx])
             add_rows(offs, a * flat + cy - 1, fault_u[a][cx:] + t_n1 * halo_n)
         o = [offs[pl.ds(a * flat, flat), :].reshape(cx, cy, nz) for a in range(3)]
-        ys[it + 1, 0] = y[0] - (o[0] - w_v[0] * o[1] - w_v[1] * o[2])
-        ys[it + 1, 1] = y[1] - o[1]
-        ys[it + 1, 2] = y[2] - o[2]
-
-    count = red_y.shape[1]
-    lines = []
-    for left, right in PAIRS:
-        lines.append(
-            jnp.sum(jnp.sum(ys[left] * ys[right], axis=(0, 1)), axis=0, keepdims=True)
-        )
-    lines.append(jnp.zeros((count - len(PAIRS), nz), jnp.float32))
-    red_y[gy] = jnp.concatenate(lines, axis=0)
-    around = [
-        remote(red_y.at[gy], red_y.at[gy], sy.at[d], ry.at[d], {"gy": lax.rem(gy + d, ny)})
-        for d in range(1, ny)
-    ]
-    for copy in around:
-        copy.start()
-    for copy in around:
-        copy.wait_recv()
-    partial = red_y[0]
-    for d in range(1, ny):
-        partial = partial + red_y[d]
-    red_x[gx] = partial
-    across = [
-        remote(red_x.at[gx], red_x.at[gx], sx.at[d], rx.at[d], {"gx": lax.rem(gx + d, nx)})
-        for d in range(1, nx)
-    ]
-    for copy in across:
-        copy.start()
-    for copy in across:
-        copy.wait_recv()
-    partial = red_x[0]
-    for d in range(1, nx):
-        partial = partial + red_x[d]
-    sums = jnp.broadcast_to(jnp.sum(partial, axis=1, keepdims=True), partial.shape)
+        ys[it + 1, 0] = o[0] - w_v[0] * o[1] - w_v[1] * o[2]
+        ys[it + 1, 1] = o[1]
+        ys[it + 1, 2] = o[2]
+
+    rows_late = [product(left, KRYLOV) for left in range(KRYLOV + 1)]
+    count = -(-len(PAIRS) // 8) * 8
+    blank = jnp.zeros((count - len(PAIRS), nz), jnp.float32)
+    table = jnp.concatenate(rows_early + rows_late + [blank], axis=0)
+    on_lane = (
+        lax.broadcasted_iota(jnp.int32, (count, nz), 0)
+        == lax.broadcasted_iota(jnp.int32, (count, nz), 1)
+    )
+
+    def to_lanes(block):
+        filled = jnp.broadcast_to(jnp.sum(block, axis=1, keepdims=True), block.shape)
+        return jnp.sum(jnp.where(on_lane, filled, 0.0), axis=0, keepdims=True)
+
+    def total_of(ref, size):
+        value = ref[0]
+        for d in range(1, size):
+            value = value + ref[d]
+        return value
+
+    line = to_lanes(table)
+    shared = []
+    if direct:
+        me = gx * ny + gy
+        red_y[me] = line
+        for dx in range(nx):
+            for dy in range(ny):
+                if dx or dy:
+                    k = dx * ny + dy
+                    target = {"gx": lax.rem(gx + dx, nx), "gy": lax.rem(gy + dy, ny)}
+                    shared.append(remote(red_y.at[me], red_y.at[me], sy.at[k], ry.at[k], target))
+        for copy in shared:
+            copy.start()
+        for copy in shared:
+            copy.wait_recv()
+        line = total_of(red_y, nx * ny)
+    else:
+        for axis, me, size, ref, send, recv in (
+            ("gy", gy, ny, red_y, sy, ry), ("gx", gx, nx, red_x, sx, rx),
+        ):
+            ref[me] = line
+            stage = [
+                remote(ref.at[me], ref.at[me], send.at[d], recv.at[d], {axis: lax.rem(me + d, size)})
+                for d in range(1, size)
+            ]
+            for copy in stage:
+                copy.start()
+            for copy in stage:
+                copy.wait_recv()
+            shared.extend(stage)
+            line = total_of(ref, size)
+    spread = jnp.where(on_lane, jnp.broadcast_to(line, (count, nz)), 0.0)
+    sums = jnp.broadcast_to(jnp.sum(spread, axis=1, keepdims=True), (count, nz))
 
     def entry(left, right):
         k = PAIRS.index((min(left, right), max(left, right)))
         return sums[k:k + 1]
 
-    normal = [[entry(a + 1, b + 1) for b in range(KRYLOV)] for a in range(KRYLOV)]
-    coefs = solve_small(normal, [entry(0, a + 1) for a in range(KRYLOV)])
+    normal = [
+        [(entry(a, b) - entry(a, b + 1)) - (entry(a + 1, b) - entry(a + 1, b + 1)) for b in range(KRYLOV)]
+        for a in range(KRYLOV)
+    ]
+    coefs = solve_small(normal, [entry(0, a) - entry(0, a + 1) for a in range(KRYLOV)])
+    left_over = [1.0 - coefs[0]] + [coefs[k] - coefs[k + 1] for k in range(KRYLOV - 1)] + [coefs[-1]]
     coefs = [c.reshape(1, 1, nz) for c in coefs]
+    left_over = [c.reshape(1, 1, nz) for c in left_over]
     mixed = []
     for c in range(3):
         combined = coefs[0] * ys[0, c]
-        applied = coefs[0] * ys[1, c]
+        rest = left_over[0] * ys[0, c]
         for k in range(1, KRYLOV):
             combined = combined + coefs[k] * ys[k, c]
-            applied = applied + coefs[k] * ys[k + 1, c]
+            rest = rest + left_over[k] * ys[k, c]
         mixed.append(combined)
-        out_o[c] = ys[0, c] - applied
+        out_o[c] = rest + left_over[KRYLOV] * ys[KRYLOV, c]
     for c in range(3):
         upd_o[c] = inv[c, 0] * mixed[0] + inv[c, 1] * mixed[1] + inv[c, 2] * mixed[2]
     for group in pending:
         sent(*group)
-    for copy in around + across:
+    for copy in shared:
         copy.wait_send()
 
 
@@ -382,7 +423,8 @@
         cap = fault_near.shape[-1]
         wells = well_cells.shape[-1]
         flat = cx * cy
-        lines = -(-len(PAIRS) // 8) * 8
+        direct = nx <= KRYLOV + 2 and nx * ny <= 64
+        stages = (nx * ny if direct else ny, nx)
         f32, i32, bf16 = jnp.float32, jnp.int32, jnp.bfloat16
         vm = pltpu.VMEM
         dma = pltpu.SemaphoreType.DMA
@@ -390,6 +432,7 @@
             vm((3, cx, cy, nz), f32), vm((3, 3, cx, cy, nz), f32), vm((3, 3, cx, cy, nz), f32),
             vm((3, cx, cy, nz), f32),
             vm((1, cap), i32), vm((1, cap), i32), vm((1, cap), f32),
+            pltpu.SMEM((1, wells), i32), pltpu.SMEM((1, wells), f32),
             vm((1, cap), i32), vm((1, cap), f32), vm((1, cap), i32),
         ]
         scratch += [vm((cx, nz), f32)] * 4 + [vm((cy, nz), f32)] * 2
@@ -401,19 +444,18 @@
         scratch += [vm((KRYLOV, 6 * cx, nz), f32)] * 2 + [vm((KRYLOV, 3, cy, nz), f32)] * 2
         scratch += [vm((KRYLOV, 6 * cx, nz), f32)] * 2 + [vm((KRYLOV, 3, cy, nz), f32)] * 2
         scratch += [vm((nz, cap), bf16)] * 4
-        scratch += [vm((ny, lines, nz), f32), vm((nx, lines, nz), f32)]
+        scratch += [vm((stages[0], 1, nz), f32), vm((stages[1], 1, nz), f32)]
         scratch += [
-            dma((7,)), dma((7,)), dma((7,)), dma((KRYLOV, 4)), dma((KRYLOV, 4)),
-            dma((ny,)), dma((ny,)), dma((nx,)), dma((nx,)),
+            dma((9,)), dma((7,)), dma((7,)), dma((KRYLOV, 4)), dma((KRYLOV, 4)),
+            dma((stages[0],)), dma((stages[0],)), dma((stages[1],)), dma((stages[1],)),
         ]
         anywhere = pl.BlockSpec(memory_space=pl.ANY)
-        scalars = pl.BlockSpec(memory_space=pltpu.SMEM)
         inside = pl.BlockSpec(memory_space=pltpu.VMEM)
         shape = jax.ShapeDtypeStruct(residual_in.shape, f32)
         return pl.pallas_call(
-            functools.partial(kernel, nx, ny, cx, cy, nz, cap, wells),
+            functools.partial(kernel, nx, ny, cx, cy, nz, cap, wells, direct),
             out_shape=(shape, shape),
-            in_specs=[anywhere] * 7 + [scalars] * 2,
+            in_specs=[anywhere] * 9,
             out_specs=(inside, inside),
             scratch_shapes=scratch,
             compiler_params=pltpu.CompilerParams(collective_id=0, has_side_effects=True),

time: 30.6 us -> 27.7 us (0.905)
  Pallas kernels: 27.6 us -> 24.7 us
    pallas_call x1, Pallas kernels: 27.6 us -> 24.7 us  [shards(): pl.pallas_call(functools.partial(kernel, nx, ny, cx, cy, nz, cap, wells,...]
where the time goes in v1:
time: 27.7 us; the launch traced here: 27.5 us
  Pallas kernels  24.7 us (89%)
  local copies, waits for them, and re-layouts  2.22 us (8%)
  between operations  0.65 us (2%)
    pallas_call x1, Pallas kernels, shards(): pl.pallas_call(functools.partial(kernel, nx, ny, cx, cy, nz, cap, wells,...  24.7 us
    unnamed x4, local copies, waits for them, and re-layouts  2.22 us

profile of v1, /device:TPU:0, one launch (start us, length us, event | category | flops | bytes accessed | tf_op | source)
XLA Modules:
  0.0 27.5 jit_solution(7434004286536784241)
XLA Ops:
  0.6 24.7 %newton.1 = (f32[3,8,8,128]{3,2,1,0:T(8,128)}, f32[3,8,8,128]{3,2,1,0:T(8,128)}) custom-call(f32[3,8,8,128]{3,2,1,0:T(8,128)} %res_h.1, f32[3,3,8,8,128]{4,3,2,1,0:T(8,128)} %acc_h.1, f32[3,3,8,8,128]{4,3,2,1,0:T(8,128)} %mob_h.1, f32[3,8,8,128]{3,2,1,0:T(8,128)} %perm_h.1, s32[1,1024]{1,0:T(1,128)} %bitcast.5, s32[1,1024]{1,0:T(1,128)} %bitcast.6, ...), custom_call_target="tpu_custom_call" | custom-call | tf_op jit(solution)/shard_map/newton/pallas_call | solution.py:455
  25.3 0.0 copy-start
  25.3 1.6 %copy.13 = f32[3,8,8,128]{3,2,1,0:T(8,128)} copy(f32[3,8,8,128]{3,2,1,0:T(8,128)} %get-tuple-element.4) | data formatting | bytes 196608
  26.9 0.0 copy-done
  26.9 0.6 %copy.14 = f32[3,8,8,128]{3,2,1,0:T(8,128)} copy(f32[3,8,8,128]{3,2,1,0:T(8,128)S(1)} %copy-done) | data formatting | bytes 196608
Async XLA Ops:
  25.3 1.6 %copy-start = (f32[3,8,8,128]{3,2,1,0:T(8,128)S(1)}, f32[3,8,8,128]{3,2,1,0:T(8,128)}, u32[]{:S(2)}) copy-start(f32[3,8,8,128]{3,2,1,0:T(8,128)} %get-tuple-element.5) | copy-start | bytes 294916

commit v2 on v1

--- a/solution.py
+++ b/solution.py
@@ -57,12 +57,23 @@
     tot, inv, mix, w_v, ys, flux, offs,
     send_u, send_l, send_e, send_w, recv_l, recv_u, recv_w, recv_e,
     z_far, z_near, z_near_l, z_far_u,
+    m_far, m_near, m_near_l, m_far_u,
     red_y, red_x,
     load_sem, s0, r0, s1, r1, sy, ry, sx, rx,
 ):
     gx, gy = lax.axis_index("gx"), lax.axis_index("gy")
     has_l, has_u = gy > 0, gy < ny - 1
     has_w, has_e = gx > 0, gx < nx - 1
+
+    loads = []
+    for k, (src, dst) in enumerate([
+        (perm_h, perm_v), (near_h, near_v), (far_h, far_v), (tr_h, tr_v),
+        (acc_h, acc_v), (mob_h, mob_v), (res_h, res_v),
+        (wc_h, wc_ref), (wr_h, wr_ref),
+    ]):
+        copy = pltpu.make_async_copy(src, dst, load_sem.at[k])
+        copy.start()
+        loads.append(copy)
 
     barrier = pltpu.get_barrier_semaphore()
     for d in range(1, ny):
@@ -78,16 +89,6 @@
             pl.semaphore_signal(barrier, inc=1, device_id={"gx": lax.rem(gx + d, nx)}, device_id_type=MESH)
         greeted = nx + ny - 2
 
-    loads = []
-    for k, (src, dst) in enumerate([
-        (perm_h, perm_v), (near_h, near_v), (far_h, far_v), (tr_h, tr_v),
-        (acc_h, acc_v), (mob_h, mob_v), (res_h, res_v),
-        (wc_h, wc_ref), (wr_h, wr_ref),
-    ]):
-        copy = pltpu.make_async_copy(src, dst, load_sem.at[k])
-        copy.start()
-        loads.append(copy)
-
     loads[0].wait()
     perm = perm_v.reshape(3 * cx * cy, nz)
     ps_u[...] = perm[pl.ds(cx * cy + cy - 1, cx, stride=cy), :]
@@ -155,23 +156,24 @@
     row_iota = lax.broadcasted_iota(jnp.int32, (rows, cap), 0)
     layer_iota = lax.broadcasted_iota(jnp.int32, (nz, cap), 0)
 
-    def slots(ref, base, onehot):
+    def slots(ref, base, onehot, mask):
         index = ref[...]
         column = quotient(index, nz)
         layer = index - column * nz
         across = quotient(column, cy)
         along = column - across * cy - base
-        onehot[...] = jnp.where(layer_iota == layer, 1.0, 0.0).astype(jnp.bfloat16)
-        return row_iota == along * cx + across
-
-    far_rows = slots(far_v, 0, z_far)
-    near_rows = slots(near_v, cy - 2, z_near)
-
-    def scatter(values, where_rows, onehot):
+        hot = jnp.where(layer_iota == layer, 1.0, 0.0).astype(jnp.bfloat16)
+        for copy in range(onehot.shape[0] // nz):
+            onehot[pl.ds(copy * nz, nz), :] = hot
+        mask[...] = jnp.where(row_iota == along * cx + across, 1.0, 0.0).astype(mask.dtype)
+
+    slots(far_v, 0, z_far, m_far)
+    slots(near_v, cy - 2, z_near, m_near)
+
+    def scatter(values, mask, onehot):
         parts = []
         for value in values:
-            chosen = jnp.where(where_rows, value, 0.0)
-            parts.extend(split_two(chosen))
+            parts.extend(mask[...] * half for half in split_two(value))
         spread = lax.dot_general(
             jnp.concatenate(parts, axis=0), onehot[...], (((1,), (1,)), ((), ())),
             preferred_element_type=jnp.float32,
@@ -181,15 +183,13 @@
             for c in range(len(values))
         ]
 
-    def gather(block, where_rows, onehot):
-        high, low = split_two(block)
+    def gather(block, mask, onehot):
         found = lax.dot_general(
-            jnp.concatenate([high, low], axis=0), onehot[...], (((1,), (0,)), ((), ())),
+            jnp.concatenate(split_two(block), axis=1), onehot[...], (((1,), (0,)), ((), ())),
             preferred_element_type=jnp.float32,
         )
-        found = found[:3 * rows] + found[3 * rows:]
         return [
-            jnp.sum(jnp.where(where_rows, found[c * rows:(c + 1) * rows], 0.0), axis=0, keepdims=True)
+            jnp.sum(mask[...] * found[c * rows:(c + 1) * rows], axis=0, keepdims=True)
             for c in range(3)
         ]
 
@@ -202,7 +202,7 @@
     t_s = jnp.where(y_iota == 0, 0.0, harmonic(perm_y, pltpu.roll(perm_y, 1, 1)))
     t_a = jnp.where(z_iota == nz - 1, 0.0, harmonic(perm_z, pltpu.roll(perm_z, nz - 1, 2)))
     t_b = jnp.where(z_iota == 0, 0.0, harmonic(perm_z, pltpu.roll(perm_z, 1, 2)))
-    far_sum = scatter([trans], far_rows, z_far)[0]
+    far_sum = scatter([trans], m_far, z_far)[0]
 
     for k in range(4, 9):
         loads[k].wait()
@@ -214,7 +214,7 @@
         rhs1 = rhs1 + jnp.where(lin == wc_ref[0, w], wr_ref[0, w], 0.0)
     arrive(first_u, first_l, first_e, first_w)
     trans_u = tr_u[...]
-    near_sum = scatter([trans_u], near_rows, z_near)[0]
+    near_sum = scatter([trans_u], m_near, z_near)[0]
     t_w0 = harmonic(perm_x[0], px_l[...])
     t_e1 = harmonic(perm_x[cx - 1], px_u[...])
     t_e = jnp.concatenate([t_x, t_e1[None]], axis=0)
@@ -290,8 +290,8 @@
         start(*copies)
         pending.append(copies)
         if it == 0:
-            near_rows_l = slots(near_l, cy - 2, z_near_l)
-            far_rows_u = slots(far_u, 0, z_far_u)
+            slots(near_l, cy - 2, z_near_l, m_near_l)
+            slots(far_u, 0, z_far_u, m_far_u)
         inner = []
         for a in range(3):
             f = field[a]
@@ -304,10 +304,10 @@
             rows_early = [product(left, right) for left, right in PAIRS if right < KRYLOV]
         arrive(*copies)
         below, above = recv_l[it], recv_u[it]
-        got_l = gather(below, near_rows_l, z_near_l)
-        got_u = gather(above, far_rows_u, z_far_u)
-        fault_l = scatter([trans * g for g in got_l], far_rows, z_far)
-        fault_u = scatter([trans_u * g for g in got_u], near_rows, z_near)
+        got_l = gather(below, m_near_l, z_near_l)
+        got_u = gather(above, m_far_u, z_far_u)
+        fault_l = scatter([trans * g for g in got_l], m_far, z_far)
+        fault_u = scatter([trans_u * g for g in got_u], m_near, z_near)
         for a in range(3):
             f = field[a]
             value = (
@@ -409,6 +409,17 @@
         copy.wait_send()
 
 
+def put_out(update_v, rest_v, update_h, rest_h, sem):
+    copies = [
+        pltpu.make_async_copy(update_v, update_h, sem.at[0]),
+        pltpu.make_async_copy(rest_v, rest_h, sem.at[1]),
+    ]
+    for copy in copies:
+        copy.start()
+    for copy in copies:
+        copy.wait()
+
+
 def solution(mesh):
     nx, ny = mesh.shape["gx"], mesh.shape["gy"]
     placed = (
@@ -443,7 +454,8 @@
         ]
         scratch += [vm((KRYLOV, 6 * cx, nz), f32)] * 2 + [vm((KRYLOV, 3, cy, nz), f32)] * 2
         scratch += [vm((KRYLOV, 6 * cx, nz), f32)] * 2 + [vm((KRYLOV, 3, cy, nz), f32)] * 2
-        scratch += [vm((nz, cap), bf16)] * 4
+        scratch += [vm((nz, cap), bf16)] * 2 + [vm((2 * nz, cap), bf16)] * 2
+        scratch += [vm((2 * cx, cap), bf16)] * 2 + [vm((2 * cx, cap), f32)] * 2
         scratch += [vm((stages[0], 1, nz), f32), vm((stages[1], 1, nz), f32)]
         scratch += [
             dma((9,)), dma((7,)), dma((7,)), dma((KRYLOV, 4)), dma((KRYLOV, 4)),
@@ -451,10 +463,11 @@
         ]
         anywhere = pl.BlockSpec(memory_space=pl.ANY)
         inside = pl.BlockSpec(memory_space=pltpu.VMEM)
+        held = pltpu.VMEM(residual_in.shape, f32)
         shape = jax.ShapeDtypeStruct(residual_in.shape, f32)
-        return pl.pallas_call(
+        update, rest = pl.pallas_call(
             functools.partial(kernel, nx, ny, cx, cy, nz, cap, wells, direct),
-            out_shape=(shape, shape),
+            out_shape=(held, held),
             in_specs=[anywhere] * 9,
             out_specs=(inside, inside),
             scratch_shapes=scratch,
@@ -465,6 +478,15 @@
             fault_near.reshape(1, cap), fault_far.reshape(1, cap), fault_trans.reshape(1, cap),
             well_cells.reshape(1, wells), well_rates.reshape(1, wells),
         )
+        return pl.pallas_call(
+            put_out,
+            out_shape=(shape, shape),
+            in_specs=[anywhere] * 2,
+            out_specs=(anywhere, anywhere),
+            scratch_shapes=[dma((2,))],
+            compiler_params=pltpu.CompilerParams(vmem_limit_bytes=1 << 20),
+            name="put_out",
+        )(*(pltpu.with_memory_space_constraint(v, pltpu.MemorySpace.VMEM) for v in (update, rest)))
 
     out = P(None, "gx", "gy", None)
     return jax.shard_map(shards, mesh=mesh, in_specs=placed, out_specs=(out, out), check_vma=False)

time: 27.7 us -> 25.6 us (0.924)
  local copies, waits for them, and re-layouts: 2.22 us -> 0 us
    unnamed x4 -> x0, local copies, waits for them, and re-layouts: 2.22 us -> none
    pallas_call x0 -> x1, Pallas kernels: none -> 0.69 us  [shards(): pl.pallas_call(put_out, out_shape=(shape, shape), in_specs=[anywhere] * 2...]
    pallas_call x1, Pallas kernels: 24.7 us -> 24.1 us  [shards(): pl.pallas_call(functools.partial(kernel, nx, ny, cx, cy, nz, cap, wells,...]
where the time goes in v2:
time: 25.6 us; the launch traced here: 25.5 us
  Pallas kernels  24.8 us (97%)
  between operations  0.64 us (2%)
    pallas_call x1, Pallas kernels, shards(): pl.pallas_call(functools.partial(kernel, nx, ny, cx, cy, nz, cap, wells,...  24.1 us
    pallas_call x1, Pallas kernels, shards(): pl.pallas_call(put_out, out_shape=(shape, shape), in_specs=[anywhere] * 2...  0.69 us

profile of v2, /device:TPU:0, one launch (start us, length us, event | category | flops | bytes accessed | tf_op | source)
XLA Modules:
  0.0 25.5 jit_solution(15743566001331264669)
XLA Ops:
  0.6 24.1 %newton.1 = (f32[3,8,8,128]{3,2,1,0:T(8,128)S(1)}, f32[3,8,8,128]{3,2,1,0:T(8,128)S(1)}) custom-call(f32[3,8,8,128]{3,2,1,0:T(8,128)} %res_h.1, f32[3,3,8,8,128]{4,3,2,1,0:T(8,128)} %acc_h.1, f32[3,3,8,8,128]{4,3,2,1,0:T(8,128)} %mob_h.1, f32[3,8,8,128]{3,2,1,0:T(8,128)} %perm_h.1, s32[1,1024]{1,0:T(1,128)} %bitcast.5, s32[1,1024]{1,0:T(1,128)} %bitcast.6, ...), custom_call_target="tpu_custom_call" | custom-call | tf_op jit(solution)/shard_map/newton/pallas_call | solution.py:468
  24.8 0.7 %put_out.1 = (f32[3,8,8,128]{3,2,1,0:T(8,128)}, f32[3,8,8,128]{3,2,1,0:T(8,128)}) custom-call(f32[3,8,8,128]{3,2,1,0:T(8,128)S(1)} %get-tuple-element.4.update_v, f32[3,8,8,128]{3,2,1,0:T(8,128)S(1)} %get-tuple-element.5.rest_v), custom_call_target="tpu_custom_call" | custom-call | tf_op jit(solution)/shard_map/put_out/pallas_call | solution.py:481

commit v3 on v2

--- a/solution.py
+++ b/solution.py
@@ -50,24 +50,29 @@
     nx, ny, cx, cy, nz, cap, wells, direct,
     res_h, acc_h, mob_h, perm_h, near_h, far_h, tr_h, wc_h, wr_h,
     upd_o, out_o,
-    res_v, acc_v, mob_v, perm_v, near_v, far_v, tr_v,
+    res_v, acc_v, mob_v, perm_v, own_idx, nbr_idx, trans,
     wc_ref, wr_ref,
-    far_u, tr_u, near_l,
-    ps_u, ps_l, py_l, py_u, px_l, px_u,
+    ps, py, px_l, px_u,
     tot, inv, mix, w_v, ys, flux, offs,
-    send_u, send_l, send_e, send_w, recv_l, recv_u, recv_w, recv_e,
-    z_far, z_near, z_near_l, z_far_u,
-    m_far, m_near, m_near_l, m_far_u,
+    send_y, recv_y, send_e, send_w, recv_w, recv_e,
+    z_own, z_nbr, m_own, m_nbr,
     red_y, red_x,
     load_sem, s0, r0, s1, r1, sy, ry, sx, rx,
 ):
     gx, gy = lax.axis_index("gx"), lax.axis_index("gy")
-    has_l, has_u = gy > 0, gy < ny - 1
+    odd = lax.rem(gy, 2)
+    beyond = [gy + 1 - 2 * odd, gy - 1 + 2 * odd]
+    has_y = [jnp.logical_and(b >= 0, b < ny) for b in beyond]
+    upper = [1 - odd, odd]
+    base = [(cy - 2) * u for u in upper]
+    other_base = [(cy - 2) * (1 - u) for u in upper]
+    edge = [(cy - 1) * u for u in upper]
+    above, below = odd, 1 - odd
     has_w, has_e = gx > 0, gx < nx - 1
 
     loads = []
     for k, (src, dst) in enumerate([
-        (perm_h, perm_v), (near_h, near_v), (far_h, far_v), (tr_h, tr_v),
+        (perm_h, perm_v), (near_h, own_idx.at[above]), (far_h, own_idx.at[below]), (tr_h, trans.at[below]),
         (acc_h, acc_v), (mob_h, mob_v), (res_h, res_v),
         (wc_h, wc_ref), (wr_h, wr_ref),
     ]):
@@ -91,8 +96,8 @@
 
     loads[0].wait()
     perm = perm_v.reshape(3 * cx * cy, nz)
-    ps_u[...] = perm[pl.ds(cx * cy + cy - 1, cx, stride=cy), :]
-    ps_l[...] = perm[pl.ds(cx * cy, cx, stride=cy), :]
+    for p in range(2):
+        ps[p] = perm[pl.ds(cx * cy + edge[p], cx, stride=cy), :]
     for k in (1, 2, 3):
         loads[k].wait()
 
@@ -104,71 +109,73 @@
             device_id=target, device_id_type=MESH,
         )
 
-    up, down = {"gy": gy + 1}, {"gy": gy - 1}
     east, west = {"gx": gx + 1}, {"gx": gx - 1}
-    first_u = [
-        remote(near_v, near_l, s0.at[0], r0.at[0], up),
-        remote(ps_u, py_l, s0.at[1], r0.at[1], up),
+    across_y = [{"gy": b} for b in beyond]
+    has_far = [jnp.logical_and(h, u == 0) for h, u in zip(has_y, upper)]
+    has_near = [jnp.logical_and(h, u == 1) for h, u in zip(has_y, upper)]
+
+    first_y = [
+        [
+            (has_y[p], has_y[p], remote(own_idx.at[p], nbr_idx.at[p], s0.at[p, 0], r0.at[p, 0], across_y[p])),
+            (has_y[p], has_y[p], remote(ps.at[p], py.at[p], s0.at[p, 1], r0.at[p, 1], across_y[p])),
+            (has_far[p], has_near[p], remote(trans.at[p], trans.at[p], s0.at[p, 2], r0.at[p, 2], across_y[p])),
+        ]
+        for p in range(2)
     ]
-    first_l = [
-        remote(far_v, far_u, s0.at[2], r0.at[2], down),
-        remote(tr_v, tr_u, s0.at[3], r0.at[3], down),
-        remote(ps_l, py_u, s0.at[4], r0.at[4], down),
+    first_x = [
+        (has_e, has_w, remote(perm_v.at[0, cx - 1], px_l, s0.at[2, 0], r0.at[2, 0], east)),
+        (has_w, has_e, remote(perm_v.at[0, 0], px_u, s0.at[2, 1], r0.at[2, 1], west)),
     ]
-    first_e = [remote(perm_v.at[0, cx - 1], px_l, s0.at[5], r0.at[5], east)]
-    first_w = [remote(perm_v.at[0, 0], px_u, s0.at[6], r0.at[6], west)]
-
-    def start(to_u, to_l, to_e, to_w):
-        for flag, copies in ((has_u, to_u), (has_l, to_l), (has_e, to_e), (has_w, to_w)):
+
+    def start(group):
+        for flag, _, copy in group:
             @pl.when(flag)
-            def _(copies=copies):
-                for copy in copies:
-                    copy.start()
-
-    def arrive(to_u, to_l, to_e, to_w):
-        for flag, copies in ((has_u, to_l), (has_l, to_u), (has_e, to_w), (has_w, to_e)):
+            def _(copy=copy):
+                copy.start()
+
+    def arrive(group):
+        for _, flag, copy in group:
             @pl.when(flag)
-            def _(copies=copies):
-                for copy in copies:
-                    copy.wait_recv()
-
-    def sent(to_u, to_l, to_e, to_w):
-        for flag, copies in ((has_u, to_u), (has_l, to_l), (has_e, to_e), (has_w, to_w)):
+            def _(copy=copy):
+                copy.wait_recv()
+
+    def sent(group):
+        for flag, _, copy in group:
             @pl.when(flag)
-            def _(copies=copies):
-                for copy in copies:
-                    copy.wait_send()
-
-    start(first_u, first_l, first_e, first_w)
+            def _(copy=copy):
+                copy.wait_send()
 
     def clear(flag, *refs):
-        @pl.when(jnp.logical_not(flag))
+        @pl.when(flag)
         def _():
             for ref in refs:
                 ref[...] = jnp.zeros(ref.shape, ref.dtype)
 
-    clear(has_l, near_l, py_l, recv_l)
-    clear(has_u, far_u, tr_u, py_u, recv_u)
-    clear(has_w, px_l, recv_w)
-    clear(has_e, px_u, recv_e)
+    start(first_y[1] + first_x + first_y[0])
+
+    for p in range(2):
+        alone = jnp.logical_not(has_y[p])
+        clear(alone, nbr_idx.at[p], py.at[p], recv_y.at[p])
+        clear(jnp.logical_and(alone, upper[p] == 1), trans.at[p])
+    clear(jnp.logical_not(has_w), px_l, recv_w)
+    clear(jnp.logical_not(has_e), px_u, recv_e)
 
     rows = 2 * cx
     row_iota = lax.broadcasted_iota(jnp.int32, (rows, cap), 0)
     layer_iota = lax.broadcasted_iota(jnp.int32, (nz, cap), 0)
 
-    def slots(ref, base, onehot, mask):
+    def slots(ref, start_row, onehot, mask):
         index = ref[...]
         column = quotient(index, nz)
         layer = index - column * nz
         across = quotient(column, cy)
-        along = column - across * cy - base
+        along = column - across * cy - start_row
         hot = jnp.where(layer_iota == layer, 1.0, 0.0).astype(jnp.bfloat16)
-        for copy in range(onehot.shape[0] // nz):
-            onehot[pl.ds(copy * nz, nz), :] = hot
+        onehot[...] = hot
         mask[...] = jnp.where(row_iota == along * cx + across, 1.0, 0.0).astype(mask.dtype)
 
-    slots(far_v, 0, z_far, m_far)
-    slots(near_v, cy - 2, z_near, m_near)
+    for p in range(2):
+        slots(own_idx.at[p], base[p], z_own.at[p], m_own.at[p])
 
     def scatter(values, mask, onehot):
         parts = []
@@ -185,15 +192,15 @@
 
     def gather(block, mask, onehot):
         found = lax.dot_general(
-            jnp.concatenate(split_two(block), axis=1), onehot[...], (((1,), (0,)), ((), ())),
+            jnp.concatenate(split_two(block), axis=0), onehot[...], (((1,), (0,)), ((), ())),
             preferred_element_type=jnp.float32,
         )
+        found = found[:3 * rows] + found[3 * rows:]
         return [
             jnp.sum(mask[...] * found[c * rows:(c + 1) * rows], axis=0, keepdims=True)
             for c in range(3)
         ]
 
-    trans = tr_v[...]
     perm_x, perm_y, perm_z = perm_v[0], perm_v[1], perm_v[2]
     y_iota = lax.broadcasted_iota(jnp.int32, (cx, cy, nz), 1)
     z_iota = lax.broadcasted_iota(jnp.int32, (cx, cy, nz), 2)
@@ -202,7 +209,6 @@
     t_s = jnp.where(y_iota == 0, 0.0, harmonic(perm_y, pltpu.roll(perm_y, 1, 1)))
     t_a = jnp.where(z_iota == nz - 1, 0.0, harmonic(perm_z, pltpu.roll(perm_z, nz - 1, 2)))
     t_b = jnp.where(z_iota == 0, 0.0, harmonic(perm_z, pltpu.roll(perm_z, 1, 2)))
-    far_sum = scatter([trans], m_far, z_far)[0]
 
     for k in range(4, 9):
         loads[k].wait()
@@ -212,15 +218,11 @@
     rhs0, rhs1, rhs2 = -res_v[0], -res_v[1], -res_v[2]
     for w in range(wells):
         rhs1 = rhs1 + jnp.where(lin == wc_ref[0, w], wr_ref[0, w], 0.0)
-    arrive(first_u, first_l, first_e, first_w)
-    trans_u = tr_u[...]
-    near_sum = scatter([trans_u], m_near, z_near)[0]
+    arrive(first_x)
     t_w0 = harmonic(perm_x[0], px_l[...])
     t_e1 = harmonic(perm_x[cx - 1], px_u[...])
     t_e = jnp.concatenate([t_x, t_e1[None]], axis=0)
     t_w = jnp.concatenate([t_w0[None], t_x], axis=0)
-    t_s0 = harmonic(ps_l[...], py_l[...])
-    t_n1 = harmonic(ps_u[...], py_u[...])
 
     flat = cx * cy
     tot[...] = (t_e + t_w + t_n + t_s + t_a + t_b).reshape(flat, nz)
@@ -229,10 +231,14 @@
         place = (pl.ds(start_row, cx, stride=cy), slice(None))
         ref[place] = ref[place] + value
 
-    add_rows(tot, 0, far_sum[:cx] + t_s0)
-    add_rows(tot, 1, far_sum[cx:])
-    add_rows(tot, cy - 2, near_sum[:cx])
-    add_rows(tot, cy - 1, near_sum[cx:] + t_n1)
+    t_edge = []
+    for p in range(2):
+        arrive(first_y[p])
+        fault_sum = scatter([trans[p]], m_own.at[p], z_own.at[p])[0]
+        t_edge.append(harmonic(ps[p], py[p]))
+        add_rows(tot, base[p], fault_sum[:cx])
+        add_rows(tot, base[p] + 1, fault_sum[cx:])
+        add_rows(tot, edge[p], t_edge[p])
 
     total = tot[...].reshape(cx, cy, nz)
     mob = [[mob_v[a, b] for b in range(3)] for a in range(3)]
@@ -266,7 +272,7 @@
     def product(left, right):
         return jnp.sum(jnp.sum(ys[left] * ys[right], axis=(0, 1)), axis=0, keepdims=True)
 
-    pending = [(first_u, first_l, first_e, first_w)]
+    pending = first_x + first_y[0] + first_y[1]
     for it in range(KRYLOV):
         y = [ys[it, c] for c in range(3)]
         field = []
@@ -276,22 +282,23 @@
             flux[pl.ds(a * flat, flat), :] = value.reshape(flat, nz)
             send_e[it, a] = value[cx - 1]
             send_w[it, a] = value[0]
-        for a in range(3):
-            for r in range(2):
-                at = pl.ds((2 * a + r) * cx, cx)
-                send_u[it, at, :] = flux[pl.ds(a * flat + cy - 2 + r, cx, stride=cy), :]
-                send_l[it, at, :] = flux[pl.ds(a * flat + r, cx, stride=cy), :]
-        copies = (
-            [remote(send_u.at[it], recv_l.at[it], s1.at[it, 0], r1.at[it, 0], up)],
-            [remote(send_l.at[it], recv_u.at[it], s1.at[it, 1], r1.at[it, 1], down)],
-            [remote(send_e.at[it], recv_w.at[it], s1.at[it, 2], r1.at[it, 2], east)],
-            [remote(send_w.at[it], recv_e.at[it], s1.at[it, 3], r1.at[it, 3], west)],
-        )
-        start(*copies)
-        pending.append(copies)
+        for p in (1, 0):
+            for a in range(3):
+                for r in range(2):
+                    send_y[p, it, pl.ds((2 * a + r) * cx, cx), :] = flux[pl.ds(a * flat + base[p] + r, cx, stride=cy), :]
+        copies_y = [
+            [(has_y[p], has_y[p], remote(send_y.at[p, it], recv_y.at[p, it], s1.at[it, p], r1.at[it, p], across_y[p]))]
+            for p in range(2)
+        ]
+        copies_x = [
+            (has_e, has_w, remote(send_e.at[it], recv_w.at[it], s1.at[it, 2], r1.at[it, 2], east)),
+            (has_w, has_e, remote(send_w.at[it], recv_e.at[it], s1.at[it, 3], r1.at[it, 3], west)),
+        ]
+        start(copies_y[1] + copies_x + copies_y[0])
+        pending += copies_x + copies_y[0] + copies_y[1]
         if it == 0:
-            slots(near_l, cy - 2, z_near_l, m_near_l)
-            slots(far_u, 0, z_far_u, m_far_u)
+            for p in range(2):
+                slots(nbr_idx.at[p], other_base[p], z_nbr.at[p], m_nbr.at[p])
         inner = []
         for a in range(3):
             f = field[a]
@@ -302,12 +309,7 @@
             inner.append(near_sums)
         if it == KRYLOV - 1:
             rows_early = [product(left, right) for left, right in PAIRS if right < KRYLOV]
-        arrive(*copies)
-        below, above = recv_l[it], recv_u[it]
-        got_l = gather(below, m_near_l, z_near_l)
-        got_u = gather(above, m_far_u, z_far_u)
-        fault_l = scatter([trans * g for g in got_l], m_far, z_far)
-        fault_u = scatter([trans_u * g for g in got_u], m_near, z_near)
+        arrive(copies_x)
         for a in range(3):
             f = field[a]
             value = (
@@ -316,12 +318,16 @@
                 + t_w * jnp.concatenate([recv_w[it, a][None], f[:-1]], axis=0)
             )
             offs[pl.ds(a * flat, flat), :] = value.reshape(flat, nz)
-            halo_s = below[(2 * a + 1) * cx:(2 * a + 2) * cx]
-            halo_n = above[2 * a * cx:(2 * a + 1) * cx]
-            add_rows(offs, a * flat, fault_l[a][:cx] + t_s0 * halo_s)
-            add_rows(offs, a * flat + 1, fault_l[a][cx:])
-            add_rows(offs, a * flat + cy - 2, fault_u[a][:cx])
-            add_rows(offs, a * flat + cy - 1, fault_u[a][cx:] + t_n1 * halo_n)
+        for p in range(2):
+            arrive(copies_y[p])
+            got = gather(recv_y[p, it], m_nbr.at[p], z_nbr.at[p])
+            fault = scatter([trans[p] * g for g in got], m_own.at[p], z_own.at[p])
+            for a in range(3):
+                at = pl.multiple_of((2 * a + 1 - upper[p]) * cx, cx)
+                halo = recv_y[p, it, pl.ds(at, cx), :]
+                add_rows(offs, a * flat + base[p], fault[a][:cx])
+                add_rows(offs, a * flat + base[p] + 1, fault[a][cx:])
+                add_rows(offs, a * flat + edge[p], t_edge[p] * halo)
         o = [offs[pl.ds(a * flat, flat), :].reshape(cx, cy, nz) for a in range(3)]
         ys[it + 1, 0] = o[0] - w_v[0] * o[1] - w_v[1] * o[2]
         ys[it + 1, 1] = o[1]
@@ -403,8 +409,7 @@
         out_o[c] = rest + left_over[KRYLOV] * ys[KRYLOV, c]
     for c in range(3):
         upd_o[c] = inv[c, 0] * mixed[0] + inv[c, 1] * mixed[1] + inv[c, 2] * mixed[2]
-    for group in pending:
-        sent(*group)
+    sent(pending)
     for copy in shared:
         copy.wait_send()
 
@@ -442,23 +447,20 @@
         scratch = [
             vm((3, cx, cy, nz), f32), vm((3, 3, cx, cy, nz), f32), vm((3, 3, cx, cy, nz), f32),
             vm((3, cx, cy, nz), f32),
-            vm((1, cap), i32), vm((1, cap), i32), vm((1, cap), f32),
+            vm((2, 1, cap), i32), vm((2, 1, cap), i32), vm((2, 1, cap), f32),
             pltpu.SMEM((1, wells), i32), pltpu.SMEM((1, wells), f32),
-            vm((1, cap), i32), vm((1, cap), f32), vm((1, cap), i32),
-        ]
-        scratch += [vm((cx, nz), f32)] * 4 + [vm((cy, nz), f32)] * 2
+        ]
+        scratch += [vm((2, cx, nz), f32)] * 2 + [vm((cy, nz), f32)] * 2
         scratch += [
             vm((flat, nz), f32), vm((3, 3, cx, cy, nz), f32), vm((3, 3, cx, cy, nz), f32),
             vm((2, cx, cy, nz), f32), vm((KRYLOV + 1, 3, cx, cy, nz), f32),
             vm((3 * flat, nz), f32), vm((3 * flat, nz), f32),
         ]
-        scratch += [vm((KRYLOV, 6 * cx, nz), f32)] * 2 + [vm((KRYLOV, 3, cy, nz), f32)] * 2
-        scratch += [vm((KRYLOV, 6 * cx, nz), f32)] * 2 + [vm((KRYLOV, 3, cy, nz), f32)] * 2
-        scratch += [vm((nz, cap), bf16)] * 2 + [vm((2 * nz, cap), bf16)] * 2
-        scratch += [vm((2 * cx, cap), bf16)] * 2 + [vm((2 * cx, cap), f32)] * 2
+        scratch += [vm((2, KRYLOV, 6 * cx, nz), f32)] * 2 + [vm((KRYLOV, 3, cy, nz), f32)] * 4
+        scratch += [vm((2, nz, cap), bf16)] * 2 + [vm((2, 2 * cx, cap), bf16), vm((2, 2 * cx, cap), f32)]
         scratch += [vm((stages[0], 1, nz), f32), vm((stages[1], 1, nz), f32)]
         scratch += [
-            dma((9,)), dma((7,)), dma((7,)), dma((KRYLOV, 4)), dma((KRYLOV, 4)),
+            dma((9,)), dma((3, 3)), dma((3, 3)), dma((KRYLOV, 4)), dma((KRYLOV, 4)),
             dma((stages[0],)), dma((stages[0],)), dma((stages[1],)), dma((stages[1],)),
         ]
         anywhere = pl.BlockSpec(memory_space=pl.ANY)

time: 25.6 us -> 26.4 us (1.031)
  Pallas kernels: 24.8 us -> 25.6 us
    pallas_call x1, Pallas kernels: 24.1 us -> 24.9 us  [shards(): pl.pallas_call(functools.partial(kernel, nx, ny, cx, cy, nz, cap, wells,...]
where the time goes in v3:
time: 26.4 us; the launch traced here: 26.3 us
  Pallas kernels  25.6 us (97%)
  between operations  0.64 us (2%)
    pallas_call x1, Pallas kernels, shards(): pl.pallas_call(functools.partial(kernel, nx, ny, cx, cy, nz, cap, wells,...  24.9 us
    pallas_call x1, Pallas kernels, shards(): pl.pallas_call(put_out, out_shape=(shape, shape), in_specs=[anywhere] * 2...  0.69 us

profile of v3, /device:TPU:0, one launch (start us, length us, event | category | flops | bytes accessed | tf_op | source)
XLA Modules:
  0.0 26.3 jit_solution(5595338733898256806)
XLA Ops:
  0.6 24.9 %newton.1 = (f32[3,8,8,128]{3,2,1,0:T(8,128)S(1)}, f32[3,8,8,128]{3,2,1,0:T(8,128)S(1)}) custom-call(f32[3,8,8,128]{3,2,1,0:T(8,128)} %res_h.1, f32[3,3,8,8,128]{4,3,2,1,0:T(8,128)} %acc_h.1, f32[3,3,8,8,128]{4,3,2,1,0:T(8,128)} %mob_h.1, f32[3,8,8,128]{3,2,1,0:T(8,128)} %perm_h.1, s32[1,1024]{1,0:T(1,128)} %bitcast.5, s32[1,1024]{1,0:T(1,128)} %bitcast.6, ...), custom_call_target="tpu_custom_call" | custom-call | tf_op jit(solution)/shard_map/newton/pallas_call | solution.py:470
  25.6 0.7 %put_out.1 = (f32[3,8,8,128]{3,2,1,0:T(8,128)}, f32[3,8,8,128]{3,2,1,0:T(8,128)}) custom-call(f32[3,8,8,128]{3,2,1,0:T(8,128)S(1)} %get-tuple-element.4.update_v, f32[3,8,8,128]{3,2,1,0:T(8,128)S(1)} %get-tuple-element.5.rest_v), custom_call_target="tpu_custom_call" | custom-call | tf_op jit(solution)/shard_map/put_out/pallas_call | solution.py:483

commit v4 on v2

--- a/solution.py
+++ b/solution.py
@@ -185,9 +185,10 @@
 
     def gather(block, mask, onehot):
         found = lax.dot_general(
-            jnp.concatenate(split_two(block), axis=1), onehot[...], (((1,), (0,)), ((), ())),
+            jnp.concatenate(split_two(block), axis=0), onehot[...], (((1,), (0,)), ((), ())),
             preferred_element_type=jnp.float32,
         )
+        found = found[:3 * rows] + found[3 * rows:]
         return [
             jnp.sum(mask[...] * found[c * rows:(c + 1) * rows], axis=0, keepdims=True)
             for c in range(3)
@@ -454,7 +455,7 @@
         ]
         scratch += [vm((KRYLOV, 6 * cx, nz), f32)] * 2 + [vm((KRYLOV, 3, cy, nz), f32)] * 2
         scratch += [vm((KRYLOV, 6 * cx, nz), f32)] * 2 + [vm((KRYLOV, 3, cy, nz), f32)] * 2
-        scratch += [vm((nz, cap), bf16)] * 2 + [vm((2 * nz, cap), bf16)] * 2
+        scratch += [vm((nz, cap), bf16)] * 4
         scratch += [vm((2 * cx, cap), bf16)] * 2 + [vm((2 * cx, cap), f32)] * 2
         scratch += [vm((stages[0], 1, nz), f32), vm((stages[1], 1, nz), f32)]
         scratch += [

time: 25.6 us -> 25.6 us (level)
  no operation moved by 1% of the time
where the time goes in v4:
time: 25.6 us; the launch traced here: 25.4 us
  Pallas kernels  24.8 us (97%)
  between operations  0.64 us (2%)
    pallas_call x1, Pallas kernels, shards(): pl.pallas_call(functools.partial(kernel, nx, ny, cx, cy, nz, cap, wells,...  24.1 us
    pallas_call x1, Pallas kernels, shards(): pl.pallas_call(put_out, out_shape=(shape, shape), in_specs=[anywhere] * 2...  0.69 us

profile of v4, /device:TPU:0, one launch (start us, length us, event | category | flops | bytes accessed | tf_op | source)
XLA Modules:
  0.0 25.4 jit_solution(14893678911880842165)
XLA Ops:
  0.6 24.1 %newton.1 = (f32[3,8,8,128]{3,2,1,0:T(8,128)S(1)}, f32[3,8,8,128]{3,2,1,0:T(8,128)S(1)}) custom-call(f32[3,8,8,128]{3,2,1,0:T(8,128)} %res_h.1, f32[3,3,8,8,128]{4,3,2,1,0:T(8,128)} %acc_h.1, f32[3,3,8,8,128]{4,3,2,1,0:T(8,128)} %mob_h.1, f32[3,8,8,128]{3,2,1,0:T(8,128)} %perm_h.1, s32[1,1024]{1,0:T(1,128)} %bitcast.5, s32[1,1024]{1,0:T(1,128)} %bitcast.6, ...), custom_call_target="tpu_custom_call" | custom-call | tf_op jit(solution)/shard_map/newton/pallas_call | solution.py:469
  24.7 0.7 %put_out.1 = (f32[3,8,8,128]{3,2,1,0:T(8,128)}, f32[3,8,8,128]{3,2,1,0:T(8,128)}) custom-call(f32[3,8,8,128]{3,2,1,0:T(8,128)S(1)} %get-tuple-element.4.update_v, f32[3,8,8,128]{3,2,1,0:T(8,128)S(1)} %get-tuple-element.5.rest_v), custom_call_target="tpu_custom_call" | custom-call | tf_op jit(solution)/shard_map/put_out/pallas_call | solution.py:482
